TPU v7x, 32 devices: a whole 2x2x4 slice. The times are simulated.
32 devices in a mesh: seq: 8 (over y, x, core), head: 4 (over z).
Axes of the slice: x: 2, y: 2, z: 4, core: 2. Of those that a mesh axis runs over, the one named last changes fastest.
Arguments:
- out_grad: bfloat16 [2048, 4096], P('seq', 'head'), may hold values from -7.2 to 7.2
- x_in: bfloat16 [2048, 4096], P('seq', 'head'), may hold values from -6 to 6
- b_in: bfloat16 [2048, 128], P('seq'), may hold values from -2.5 to 2.5
- c_in: bfloat16 [2048, 128], P('seq'), may hold values from -2.5 to 2.5
- dt_raw: float32 [64, 2048], P('head', 'seq'), may hold values from -5.1 to -0.7
- dt_bias: float32 [64], P('head'), may hold values from -0.5 to 0.5
- a_log: float32 [64], P('head'), may hold values from -7.5 to 2.2
- d_skip: float32 [64], P('head'), may hold values from 0.5 to 1.5
- states: bfloat16 [8, 4096, 128], P('seq', 'head'), may hold values from -6 to 6
- w_out: bfloat16 [4096, 4096], P('head'), may hold values from -0.09375 to 0.09375
- w_in: bfloat16 [4096, 4096], P(None, 'head'), may hold values from -0.125 to 0.125
Outputs:
- in_grad: bfloat16 [4096, 2048], P('head', 'seq')
- bc_grad: bfloat16 [256, 2048], P('head', 'seq')
- dt_grad: float32 [64, 2048], P('head', 'seq')
- param_grad: float32 [3, 64], P(None, 'head')
All inputs are finite; a program needn't handle non-finite values.
Results may differ from a plain program's by a relative error of at most 0.015.
Values may be sent and summed in bfloat16 or wider, within the bound.
A program may use at most 64 MiB of HBM per device.

v0:
```python
import jax
import jax.numpy as jnp
from jax import lax
from jax.sharding import PartitionSpec as P


def partners(count, distance):
    return [(place, place ^ distance) for place in range(count)]


def entering(decay, state, axis):
    count, mine = (lax.axis_size(axis), lax.axis_index(axis))
    carried = jnp.zeros_like(state)
    reach = jnp.ones_like(decay)
    distance = 1
    while distance < count:
        pairs = partners(count, distance)
        other_decay = lax.ppermute(decay, axis, pairs)
        other_state = lax.ppermute(state.astype(jnp.bfloat16), axis, pairs).astype(jnp.float32)
        earlier = mine // distance % 2 == 0
        carried = jnp.where(earlier, carried + reach[:, None, None] * other_state, carried)
        reach = jnp.where(earlier, reach * other_decay, reach)
        state = jnp.where(
            earlier,
            state + decay[:, None, None] * other_state,
            other_state + other_decay[:, None, None] * state,
        )
        decay = decay * other_decay
        distance *= 2
    return carried


def summed(value, axis):
    count = lax.axis_size(axis)
    distance = 1
    while distance < count:
        value = value + lax.ppermute(value, axis, partners(count, distance))
        distance *= 2
    return value


def shards(out_grad, x_in, b_in, c_in, dt_raw, dt_bias, a_log, d_skip, states, w_out, w_in):
    tokens_here, inner_here = x_in.shape
    group_heads = dt_raw.shape[0]
    head_dim = inner_here // group_heads
    state_dim = b_in.shape[1]
    contract_last = (((1,), (1,)), ((), ()))
    head_sum = lax.dot_general(
        lax.all_gather(out_grad, "head", axis=1, tiled=True),
        w_out,
        contract_last,
        preferred_element_type=jnp.float32,
    )
    dy_heads = head_sum.astype(jnp.bfloat16).reshape(tokens_here, group_heads, head_dim)
    dy_wide = dy_heads.astype(jnp.float32)
    x_heads = x_in.reshape(tokens_here, group_heads, head_dim)
    x_wide = x_heads.astype(jnp.float32)
    decay_rate = jnp.exp(a_log)
    step_size = jax.nn.softplus(dt_raw + dt_bias[:, None])
    log_step = -decay_rate[:, None] * step_size
    cumlog = jnp.cumsum(log_step, axis=1)
    positions = jnp.arange(tokens_here)
    causal = positions[:, None] >= positions[None, :]
    log_gaps = cumlog[:, :, None] - cumlog[:, None, :]
    decay_mask = jnp.where(causal[None], jnp.exp(jnp.minimum(log_gaps, 0.0)), 0.0)
    scores = lax.dot_general(c_in, b_in, contract_last, preferred_element_type=jnp.float32)
    step_rows = step_size.T
    x_scaled = (x_wide * step_rows[:, :, None]).astype(jnp.bfloat16)
    pair_dots = jnp.einsum("ihp,jhp->hij", dy_heads, x_scaled, preferred_element_type=jnp.float32)
    kernel = (scores[None] * decay_mask).astype(jnp.bfloat16)
    intra_back = jnp.einsum("hij,ihp->jhp", kernel, dy_heads, preferred_element_type=jnp.float32)
    masked_dots = (pair_dots * decay_mask).astype(jnp.bfloat16)
    start_decay = jnp.exp(cumlog)
    dy_decay = (dy_wide * start_decay.T[:, :, None]).astype(jnp.bfloat16)
    local_state = jnp.einsum("ihp,in->hpn", dy_decay, c_in, preferred_element_type=jnp.float32)
    end_total = jnp.exp(cumlog[:, -1])
    entry_state = states.reshape(group_heads, head_dim, state_dim)
    db_intra = jnp.einsum("hij,in->nj", masked_dots, c_in, preferred_element_type=jnp.float32)
    dc_intra = jnp.einsum("hij,jn->ni", masked_dots, b_in, preferred_element_type=jnp.float32)
    dc_entry = jnp.einsum("ihp,hpn->ni", dy_decay, entry_state, preferred_element_type=jnp.float32)
    ystate = jnp.einsum("in,hpn->ihp", c_in, entry_state, preferred_element_type=jnp.float32)
    pair_weight = pair_dots * scores[None] * decay_mask
    state_terms = start_decay * jnp.sum(dy_wide * ystate, axis=2).T
    skip_terms = jnp.sum(dy_wide * x_wide, axis=(0, 2))
    carried = entering(end_total, local_state, "seq")
    carried_bf = carried.astype(jnp.bfloat16)
    state_back = jnp.einsum("jn,hpn->jhp", b_in, carried_bf, preferred_element_type=jnp.float32)
    end_decay = jnp.exp(cumlog[:, -1:] - cumlog)
    end_weight = (step_size * end_decay).T
    x_grad = (
        (
            step_rows[:, :, None] * intra_back
            + end_weight[:, :, None] * state_back
            + d_skip[None, :, None] * dy_wide
        )
        .astype(jnp.bfloat16)
        .reshape(tokens_here, inner_here)
    )
    x_end = (x_wide * end_weight[:, :, None]).astype(jnp.bfloat16)
    db_entry = jnp.einsum("jhp,hpn->nj", x_end, carried_bf, preferred_element_type=jnp.float32)
    bc_part = jnp.concatenate([db_intra + db_entry, dc_intra + dc_entry], axis=0)
    end_terms = end_weight.T * jnp.sum(x_wide * state_back, axis=2).T
    cum_grad = pair_weight.sum(axis=2) - pair_weight.sum(axis=1) + state_terms - end_terms
    tail_grad = end_terms.sum(axis=1) + end_total * jnp.sum(
        entry_state.astype(jnp.float32) * carried, axis=(1, 2)
    )
    cum_grad = cum_grad.at[:, -1].add(tail_grad)
    step_grad = jnp.cumsum(cum_grad[:, ::-1], axis=1)[:, ::-1]
    dt_sum = (
        -decay_rate[:, None] * step_grad
        + jnp.sum(x_wide * (intra_back + end_decay.T[:, :, None] * state_back), axis=2).T
    )
    dt_grad = dt_sum * jax.nn.sigmoid(dt_raw + dt_bias[:, None])
    param_terms = jnp.stack(
        [jnp.sum(step_grad * log_step, axis=1), skip_terms, jnp.sum(dt_grad, axis=1)]
    )
    heads_count = lax.axis_size("head")
    in_term = lax.dot_general(
        w_in, x_grad, contract_last, preferred_element_type=jnp.float32
    ).astype(jnp.bfloat16)
    rows_here = in_term.shape[0] // heads_count
    both = jnp.concatenate(
        [
            in_term.reshape(heads_count, rows_here, tokens_here),
            bc_part.astype(jnp.bfloat16).reshape(heads_count, -1, tokens_here),
        ],
        axis=1,
    )
    both_sum = lax.psum_scatter(
        both.reshape(-1, tokens_here), "head", scatter_dimension=0, tiled=True
    )
    in_part, bc_sum = (both_sum[:rows_here], both_sum[rows_here:])
    norm_scale = (lax.axis_size("seq") * tokens_here * head_dim) ** (-0.5)
    param_grad = summed(param_terms, "seq") * norm_scale
    return (in_part, bc_sum, dt_grad, param_grad)


def solution(mesh):
    return jax.shard_map(
        shards,
        mesh=mesh,
        in_specs=(
            P("seq", "head"),
            P("seq", "head"),
            P("seq", None),
            P("seq", None),
            P("head", "seq"),
            P("head"),
            P("head"),
            P("head"),
            P("seq", "head", None),
            P("head", None),
            P(None, "head"),
        ),
        out_specs=(P("head", "seq"), P("head", "seq"), P("head", "seq"), P(None, "head")),
        check_vma=False,
    )
```

profile of v0, /device:TPU:0, one launch (start us, length us, event | category | flops | bytes accessed | tf_op | source)
XLA Modules:
  0.0 161.3 jit_solution(2156898000324561240)
XLA Ops:
  16.4 1.3 copy.102
  17.8 3.0 %collective-permute-start.3 = (f32[16]{0:T(128)S(1)}, f32[16]{0:T(128)S(1)}, u32[]{:S(2)}, u32[]{:S(2)}) collective-permute-start(f32[16]{0:T(128)S(1)} %fusion.46), channel_id=1, source_target_pairs={{0,8},{4,12},{8,0},{12,4},{16,24},{20,28},{24,16},{28,20},{1,9},{5... | collective-permute-start | bytes 200 | tf_op jit(solution)/shard_map/ppermute | solution.py:18
  20.8 1.3 copy.103
  23.5 34.5 %all-gather.2.cloned.1.call-done = bf16[256,4096]{1,0:T(8,128)(2,1)} async-done(((bf16[256,1024]{1,0:T(8,128)(2,1)}), bf16[256,4096]{1,0:T(8,128)(2,1)}) %all-gather.2.cloned.1.call-update) | async-done | bytes 2097168 | tf_op jit(solution)/shard_map/all_gather | solution.py:49
  58.0 7.2 %fusion.16 = (f32[1024]{0:T(1024)}, bf16[256,1024]{1,0:T(8,128)(2,1)S(1)}, bf16[256,1024]{1,0:T(8,128)(2,1)S(1)}) fusion(bf16[256,1024]{1,0:T(8,128)(2,1)S(1)} %copy-done.4, f32[256,1024]{1,0:T(8,128)} %copy.103, bf16[256,4096]{1,0:T(8,128)(2,1)} %all-gather.2.cloned.1.call-done, bf16[1024,4096]{1,0:T(8,128)(2,1)} %param.22), kind=kOutput, calls=%fused_computation.34 | convolution fusion | flops 2149317632 | bytes 13111296 | tf_op jit(solution)/shard_map/dot_general | solution.py:48
  66.1 4.0 %fusion.1 = (f32[16,256]{1,0:T(8,128)}, f32[16,256]{1,0:T(8,128)}, bf16[256,256]{1,0:T(8,128)(2,1)S(1)}) fusion(f32[16,256]{1,0:T(8,128)} %copy-done.7, f32[256,256]{1,0:T(8,128)S(1)} %fusion.53, pred[256,256]{1,0:T(8,128)(4,1)} %iota_compare_fusion, bf16[256,16,64]{0,2,1:T(8,128)(2,1)S(1)} %bitcast.112, f32[256,16,64]{0,2,1:T(8,128)S(1)} %bitcast.118, ...), kind=kOutput, calls=%fused_computation.7 | convolution fusion | flops 146202624 | bytes 2097152 | tf_op jit(solution)/shard_map/ihp,jhp->hij/dot_general | solution.py:69
  70.3 1.5 collective-permute-start.2
  71.9 3.2 %fusion.9 = f32[256,16,64]{0,2,1:T(8,128)} fusion(bf16[256,16,64]{0,2,1:T(8,128)(2,1)S(1)} %bitcast.113, f32[16,256]{1,0:T(8,128)S(1)} %copy-done.8, f32[256,256]{1,0:T(8,128)} %copy-done.6, pred[256,256]{1,0:T(8,128)(4,1)S(1)} %copy-done.9), kind=kOutput, calls=%fused_computation.19 | convolution fusion | flops 139460608 | bytes 1916928 | tf_op jit(solution)/shard_map/hij,ihp->jhp/dot_general | solution.py:71
  75.1 4.0 %collective-permute-done.2 = bf16[16,64,128]{2,1,0:T(8,128)(2,1)S(1)} collective-permute-done((bf16[16,64,128]{2,1,0:T(8,128)(2,1)S(1)}, bf16[16,64,128]{2,1,0:T(8,128)(2,1)S(1)}, u32[]{:S(2)}, u32[]{:S(2)}) %collective-permute-start.2) | collective-permute-done | bytes 262176 | tf_op jit(solution)/shard_map/ppermute | solution.py:19
  79.4 1.5 collective-permute-start.4
  81.5 5.9 %collective-permute-done.4 = bf16[16,64,128]{2,1,0:T(8,128)(2,1)S(1)} collective-permute-done((bf16[16,64,128]{2,1,0:T(8,128)(2,1)S(1)}, bf16[16,64,128]{2,1,0:T(8,128)(2,1)S(1)}, u32[]{:S(2)}, u32[]{:S(2)}) %collective-permute-start.4) | collective-permute-done | bytes 262176 | tf_op jit(solution)/shard_map/ppermute | solution.py:19
  88.9 2.6 %multiply_reduce_fusion.1 = (f32[256,16]{0,1:T(8,128)}, f32[256,16]{0,1:T(8,128)}, bf16[256,16,64]{0,2,1:T(8,128)(2,1)S(1)}) fusion(f32[256,1024]{0,1:T(8,128)S(1)} %copy.102, f32[256,16,64]{0,2,1:T(8,128)} %fusion.9, f32[256,16]{0,1:T(8,128)S(1)} %copy-done.10, bf16[256,1024]{0,1:T(8,128)(2,1)S(1)} %copy.94, f32[16]{0:T(128)} %param.20, ...), kind=kOutput, calls=%fused_computation.39 | convolution fusion | flops 71950336 | bytes 4079811 | tf_op jit(solution)/shard_map/jn,hpn->jhp/dot_general | solution.py:87
  91.6 5.8 %fusion = bf16[4096,256]{0,1:T(8,128)(2,1)S(1)} fusion(bf16[256,1024]{0,1:T(8,128)(2,1)S(1)} %bitcast.133, bf16[4096,1024]{1,0:T(8,128)(2,1)} %param.23), kind=kOutput, calls=%fused_computation.1 | convolution fusion | flops 2148532224 | bytes 11010048 | tf_op jit(solution)/shard_map/dot_general | solution.py:118
  97.4 2.8 %reshape.138 = bf16[4,1024,256]{1,0,2:T(4,128)(2,1)} reshape(bf16[4096,256]{0,1:T(8,128)(2,1)S(1)} %fusion) | data formatting | bytes 4194304 | tf_op jit(solution)/shard_map/reshape | solution.py:124
  100.2 2.8 %pad_maximum_fusion = bf16[4,1088,256]{1,0,2:T(4,128)(2,1)S(1)} fusion(bf16[4,64,256]{1,0,2:T(4,128)(2,1)} %copy.105, bf16[4,1024,256]{1,0,2:T(4,128)(2,1)} %reshape.138), kind=kLoop, calls=%fused_computation.9 | loop fusion | flops 4456448 | bytes 4456448 | tf_op jit(solution)/shard_map/concatenate | solution.py:122
  103.0 3.6 %copy.106 = bf16[4,1088,256]{2,1,0:T(8,128)(2,1)} copy(bf16[4,1088,256]{1,0,2:T(4,128)(2,1)S(1)} %pad_maximum_fusion) | data formatting | bytes 4456448 | tf_op jit(solution)/shard_map/concatenate | solution.py:122
  110.6 1.6 %multiply_reduce_fusion.2 = f32[16]{0:T(128)S(1)} fusion(bf16[16,64,128]{2,1,0:T(8,128)(2,1)} %bitcast.116, bf16[16,64,128]{2,1,0:T(8,128)(2,1)} %copy-done.5, f32[16]{0:T(128)} %get-tuple-element.35, bf16[16,64,128]{2,1,0:T(8,128)(2,1)} %copy-done.2, f32[16]{0:T(128)} %get-tuple-element.36, bf16[16,64,128]{2,1,0:T(8,128)(2,1)S(1)} %collective-permute-done, ...), kind=kLoop, calls=%fused_computation.57 | loop fusion | flops 1703920 | bytes 1048771 | tf_op jit(solution)/shard_map/reduce_sum | solution.py:104
  115.1 1.4 collective-permute-start.6
  116.5 2.2 %collective-permute-done.6 = f32[3,16]{1,0:T(4,128)S(1)} collective-permute-done((f32[3,16]{1,0:T(4,128)S(1)}, f32[3,16]{1,0:T(4,128)S(1)}, u32[]{:S(2)}, u32[]{:S(2)}) %collective-permute-start.6) | collective-permute-done | bytes 224 | tf_op jit(solution)/shard_map/ppermute | solution.py:37
  118.8 1.4 collective-permute-start.7
  120.9 1.6 collective-permute-done.7
  123.0 28.2 %reduce-scatter.2.cloned.1.call-done = bf16[1088,256]{1,0:T(8,128)(2,1)} async-done(((bf16[4352,256]{1,0:T(8,128)(2,1)}), bf16[1088,256]{1,0:T(8,128)(2,1)}) %reduce-scatter.2.cloned.1.call-update) | async-done | bytes 557072 | tf_op jit(solution)/shard_map/reduce_scatter | solution.py:129
  151.2 1.4 slice.50
  152.6 1.9 %slice.49 = bf16[1024,256]{1,0:T(8,128)(2,1)} slice(bf16[1088,256]{1,0:T(8,128)(2,1)} %reduce-scatter.2.cloned.1.call-done), slice={[0:1024], [0:256]} | slice | bytes 1048576 | tf_op jit(solution)/shard_map/slice | solution.py:132
  (128 shorter events, 22.1 us)
Async XLA Ops:
  7.2 8.2 %copy-start = (bf16[256,128]{1,0:T(8,128)(2,1)S(1)}, bf16[256,128]{1,0:T(8,128)(2,1)}, u32[]{:S(2)}) copy-start(bf16[256,128]{1,0:T(8,128)(2,1)} %param.15) | copy-start | bytes 196612
  7.2 50.8 %copy-start.4 = (bf16[256,1024]{1,0:T(8,128)(2,1)S(1)}, bf16[256,1024]{1,0:T(8,128)(2,1)}, u32[]{:S(2)}) copy-start(bf16[256,1024]{1,0:T(8,128)(2,1)} %param.14) | copy-start | bytes 1572868
  7.2 50.8 %all-gather.2.cloned.1.call-start = ((), (), s32[]{:S(2)}) async-start(), calls=%async_computation.1 | async-start | bytes 2621440 | tf_op jit(solution)/shard_map/all_gather | solution.py:49
  7.9 143.3 %reduce-scatter.2.cloned.1.call-start = ((), (), s32[]{:S(2)}) async-start(), calls=%async_computation.2 | async-start | bytes 2785280 | tf_op jit(solution)/shard_map/reduce_scatter | solution.py:129
  11.3 11.0 %copy-start.19 = (f32[16]{0:T(128)}, f32[16]{0:T(128)S(1)}, u32[]{:S(2)}) copy-start(f32[16]{0:T(128)S(1)} %fusion.45) | copy-start | bytes 196
  11.3 6.5 %collective-permute-start.1 = (f32[16]{0:T(128)S(1)}, f32[16]{0:T(128)S(1)}, u32[]{:S(2)}, u32[]{:S(2)}) collective-permute-start(f32[16]{0:T(128)S(1)} %fusion.45), channel_id=1, source_target_pairs={{0,4},{4,0},{8,12},{12,8},{16,20},{20,16},{24,28},{28,24},{1,5},{5... | collective-permute-start | bytes 200 | tf_op jit(solution)/shard_map/ppermute | solution.py:18
  16.4 49.7 %copy-start.6 = (f32[256,256]{1,0:T(8,128)}, f32[256,256]{1,0:T(8,128)S(1)}, u32[]{:S(2)}) copy-start(f32[256,256]{1,0:T(8,128)S(1)} %fusion.53) | copy-start | bytes 786436
  17.8 4.5 %collective-permute-start.3 = (f32[16]{0:T(128)S(1)}, f32[16]{0:T(128)S(1)}, u32[]{:S(2)}, u32[]{:S(2)}) collective-permute-start(f32[16]{0:T(128)S(1)} %fusion.46), channel_id=1, source_target_pairs={{0,8},{4,12},{8,0},{12,4},{16,24},{20,28},{24,16},{28,20},{1,9},{5... | collective-permute-start | bytes 200 | tf_op jit(solution)/shard_map/ppermute | solution.py:18
  23.5 42.2 %copy-start.3 = (bf16[256,128]{1,0:T(8,128)(2,1)S(1)}, bf16[256,128]{1,0:T(8,128)(2,1)}, u32[]{:S(2)}) copy-start(bf16[256,128]{1,0:T(8,128)(2,1)} %param.16) | copy-start | bytes 196612
  65.9 4.1 %collective-permute-start = (bf16[16,64,128]{2,1,0:T(8,128)(2,1)S(1)}, bf16[16,64,128]{2,1,0:T(8,128)(2,1)S(1)}, u32[]{:S(2)}, u32[]{:S(2)}) collective-permute-start(bf16[16,64,128]{2,1,0:T(8,128)(2,1)S(1)} %get-tuple-element.48), channel_id=1, source_target_pairs={{0,4},{4,0},{8,12},{12,8},{16,20},{20,16},{24,28},{28,24},{1,5},{5... | collective-permute-start | bytes 786440 | tf_op jit(solution)/shard_map/ppermute | solution.py:19
  70.1 9.0 %copy-start.24 = (f32[16]{0:T(128)S(1)}, f32[16]{0:T(128)}, u32[]{:S(2)}) copy-start(f32[16]{0:T(128)} %copy-done.23) | copy-start | bytes 196
  70.1 9.0 %copy-start.28 = (f32[16]{0:T(128)S(1)}, f32[16]{0:T(128)}, u32[]{:S(2)}) copy-start(f32[16]{0:T(128)} %copy-done.27) | copy-start | bytes 196
  70.3 10.7 %copy-start.1 = (bf16[1,1024,128]{2,1,0:T(8,128)(2,1)S(1)}, bf16[1,1024,128]{2,1,0:T(8,128)(2,1)}, u32[]{:S(2)}) copy-start(bf16[1,1024,128]{2,1,0:T(8,128)(2,1)} %param.21) | copy-start | bytes 786436
  70.3 17.0 %copy-start.11 = (f32[256,16]{0,1:T(8,128)S(1)}, f32[256,16]{0,1:T(8,128)}, u32[]{:S(2)}) copy-start(f32[256,16]{0,1:T(8,128)} %copy.99) | copy-start | bytes 49156
  70.3 17.0 %copy-start.17 = (f32[16]{0:T(128)S(1)}, f32[16]{0:T(128)}, u32[]{:S(2)}) copy-start(f32[16]{0:T(128)} %get-tuple-element.35) | copy-start | bytes 196
  70.3 17.0 %copy-start.18 = (f32[16]{0:T(128)S(1)}, f32[16]{0:T(128)}, u32[]{:S(2)}) copy-start(f32[16]{0:T(128)} %get-tuple-element.36) | copy-start | bytes 196
  70.3 8.8 %collective-permute-start.2 = (bf16[16,64,128]{2,1,0:T(8,128)(2,1)S(1)}, bf16[16,64,128]{2,1,0:T(8,128)(2,1)S(1)}, u32[]{:S(2)}, u32[]{:S(2)}) collective-permute-start(bf16[16,64,128]{2,1,0:T(8,128)(2,1)S(1)} %fusion.48), channel_id=1, source_target_pairs={{0,8},{4,12},{8,0},{12,4},{16,24},{20,28},{24,16},{28,20},{1,9},{5... | collective-permute-start | bytes 786440 | tf_op jit(solution)/shard_map/ppermute | solution.py:19
  75.1 13.8 %copy-start.10 = (f32[256,16]{0,1:T(8,128)S(1)}, f32[256,16]{0,1:T(8,128)}, u32[]{:S(2)}) copy-start(f32[256,16]{0,1:T(8,128)} %copy.114) | copy-start | bytes 49156
  79.1 12.4 %copy-start.2 = (bf16[16,64,128]{2,1,0:T(8,128)(2,1)}, bf16[16,64,128]{2,1,0:T(8,128)(2,1)S(1)}, u32[]{:S(2)}) copy-start(bf16[16,64,128]{2,1,0:T(8,128)(2,1)S(1)} %collective-permute-done.2) | copy-start | bytes 786436
  79.4 7.9 %collective-permute-start.4 = (bf16[16,64,128]{2,1,0:T(8,128)(2,1)S(1)}, bf16[16,64,128]{2,1,0:T(8,128)(2,1)S(1)}, u32[]{:S(2)}, u32[]{:S(2)}) collective-permute-start(bf16[16,64,128]{2,1,0:T(8,128)(2,1)S(1)} %fusion.24), channel_id=1, source_target_pairs={{0,16},{4,20},{8,24},{12,28},{16,0},{20,4},{24,8},{28,12},{1,17},{... | collective-permute-start | bytes 786440 | tf_op jit(solution)/shard_map/ppermute | solution.py:19
  87.3 10.0 %copy-start.5 = (bf16[16,64,128]{2,1,0:T(8,128)(2,1)}, bf16[16,64,128]{2,1,0:T(8,128)(2,1)S(1)}, u32[]{:S(2)}) copy-start(bf16[16,64,128]{2,1,0:T(8,128)(2,1)S(1)} %collective-permute-done.4) | copy-start | bytes 786436
  113.9 1.2 collective-permute-start.5
  115.1 3.7 %collective-permute-start.6 = (f32[3,16]{1,0:T(4,128)S(1)}, f32[3,16]{1,0:T(4,128)S(1)}, u32[]{:S(2)}, u32[]{:S(2)}) collective-permute-start(f32[3,16]{1,0:T(4,128)S(1)} %fusion.47), channel_id=1, source_target_pairs={{0,8},{4,12},{8,0},{12,4},{16,24},{20,28},{24,16},{28,20},{1,9},{5... | collective-permute-start | bytes 584 | tf_op jit(solution)/shard_map/ppermute | solution.py:37
  118.8 3.7 %collective-permute-start.7 = (f32[3,16]{1,0:T(4,128)S(1)}, f32[3,16]{1,0:T(4,128)S(1)}, u32[]{:S(2)}, u32[]{:S(2)}) collective-permute-start(f32[3,16]{1,0:T(4,128)S(1)} %fusion.69), channel_id=1, source_target_pairs={{0,16},{4,20},{8,24},{12,28},{16,0},{20,4},{24,8},{28,12},{1,17},{... | collective-permute-start | bytes 584 | tf_op jit(solution)/shard_map/ppermute | solution.py:37
  (15 other events, 66.4 us)
Sparse Core Ops, SparseCore 0:
  9.6 48.3 all-gather.1
  106.7 44.4 reduce-scatter.1
where the time goes:
time: 162 us; the launch traced here: 161 us
  waiting for transfers between devices  78.4 us (48%)
  matrix products  26.6 us (16%)
  local copies, waits for them, and re-layouts  21.4 us (13%)
  between operations  14.4 us (9%)
  other arithmetic  10.9 us (7%)
  starting transfers between devices  9.59 us (6%)
    all_gather x1, waiting for transfers between devices, shards(): lax.all_gather(out_grad, 'head', axis=1, tiled=True)  34.5 us
    reduce_scatter x1, waiting for transfers between devices, shards(): lax.psum_scatter(both.reshape(-1, tokens_here), 'head', scatter_dimension...  28.2 us
    ppermute x3, waiting for transfers between devices, entering(): lax.ppermute(state.astype(jnp.bfloat16), axis, pairs).astype(jnp.float32)  9.91 us
    dot_general x1, matrix products, shards(): lax.dot_general(lax.all_gather(out_grad, 'head', axis=1, tiled=True), w_o...  7.21 us
    dot_general x1, matrix products, shards(): lax.dot_general(w_in, x_grad, contract_last, preferred_element_type=jnp.f...  5.8 us
    ppermute x3, waiting for transfers between devices, summed(): value = value + lax.ppermute(value, axis, partners(count, distance))  4.97 us
    dot_general x1, matrix products, shards(): jnp.einsum('ihp,jhp->hij', dy_heads, x_scaled, preferred_element_type=jnp...  4 us
    concatenate x1, local copies, waits for them, and re-layouts, shards(): jnp.concatenate([in_term.reshape(heads_count, rows_here, tokens_here), bc...  3.55 us
  transfers between devices with their start and end apart: 10, of which 8 were waited for; matrix products, arithmetic and copies ran while one was open for 17% of the time, Pallas kernels for 0%

commit v1 on v0

--- a/solution.py
+++ b/solution.py
@@ -2,6 +2,18 @@
 import jax.numpy as jnp
 from jax import lax
 from jax.sharding import PartitionSpec as P
+
+
+def gather_by_bits(x, axis, dim):
+    ways, here, lap = (lax.axis_size(axis), lax.axis_index(axis), x.shape[dim])
+    line, have = (x, 1)
+    while have < ways:
+        line = jnp.concatenate(
+            [line, lax.ppermute(line, axis, [(d, (d - have) % ways) for d in range(ways)])],
+            axis=dim,
+        )
+        have = 2 * have
+    return jnp.roll(line, here * lap, axis=dim)
 
 
 def partners(count, distance):
@@ -46,7 +58,7 @@
     state_dim = b_in.shape[1]
     contract_last = (((1,), (1,)), ((), ()))
     head_sum = lax.dot_general(
-        lax.all_gather(out_grad, "head", axis=1, tiled=True),
+        gather_by_bits(out_grad, "head", 1),
         w_out,
         contract_last,
         preferred_element_type=jnp.float32,

time: 162 us -> 184 us (1.14)
  local copies, waits for them, and re-layouts: 21.4 us -> 30.9 us
  other arithmetic: 10.9 us -> 16.9 us
  starting transfers between devices: 9.59 us -> 14.4 us
  waiting for transfers between devices: 78.4 us -> 81.2 us
    ppermute x0 -> x2, waiting for transfers between devices: none -> 34.9 us  [gather_by_bits(): lax.ppermute(line, axis, [(d, (d - have) % ways) for d in range(ways)])]
    all_gather x1 -> x0, waiting for transfers between devices: 34.5 us -> none  [shards(): lax.all_gather(out_grad, 'head', axis=1, tiled=True)]
    ppermute x0 -> x2, starting transfers between devices: none -> 6.49 us  [gather_by_bits(): lax.ppermute(line, axis, [(d, (d - have) % ways) for d in range(ways)])]
    unnamed x60 -> x57, local copies, waits for them, and re-layouts: 2.2 us -> 6.76 us
    concatenate x0 -> x1, other arithmetic: none -> 2.14 us  [gather_by_bits(): jnp.concatenate([line, lax.ppermute(line, axis, [(d, (d - have) % ways) f...]
    ppermute x2, waiting for transfers between devices: 0.15 us -> 2.24 us  [entering(): other_decay = lax.ppermute(decay, axis, pairs)]
    ppermute x2, starting transfers between devices: 3.51 us -> 1.49 us  [entering(): other_decay = lax.ppermute(decay, axis, pairs)]
  transfers between devices with their start and end apart: 10 -> 11, of which waited for: 8 -> 9; matrix products, arithmetic and copies ran while one was open for 17% -> 20% of each run, Pallas kernels for 0% -> 0%
where the time goes in v1:
time: 184 us; the launch traced here: 183 us
  waiting for transfers between devices  81.2 us (44%)
  local copies, waits for them, and re-layouts  30.9 us (17%)
  matrix products  25.5 us (14%)
  other arithmetic  16.9 us (9%)
  starting transfers between devices  14.4 us (8%)
  between operations  14.3 us (8%)
    ppermute x2, waiting for transfers between devices, gather_by_bits(): lax.ppermute(line, axis, [(d, (d - have) % ways) for d in range(ways)])  34.9 us
    reduce_scatter x1, waiting for transfers between devices, shards(): lax.psum_scatter(both.reshape(-1, tokens_here), 'head', scatter_dimension...  28.7 us
    ppermute x3, waiting for transfers between devices, entering(): lax.ppermute(state.astype(jnp.bfloat16), axis, pairs).astype(jnp.float32)  10.7 us
    dot_general x1, matrix products, shards(): lax.dot_general(gather_by_bits(out_grad, 'head', 1), w_out, contract_last...  7.1 us
    unnamed x57, local copies, waits for them, and re-layouts  6.76 us
    ppermute x2, starting transfers between devices, gather_by_bits(): lax.ppermute(line, axis, [(d, (d - have) % ways) for d in range(ways)])  6.49 us
    dot_general x1, matrix products, shards(): lax.dot_general(w_in, x_grad, contract_last, preferred_element_type=jnp.f...  5.81 us
    ppermute x3, waiting for transfers between devices, summed(): value = value + lax.ppermute(value, axis, partners(count, distance))  4.66 us
  transfers between devices with their start and end apart: 11, of which 9 were waited for; matrix products, arithmetic and copies ran while one was open for 20% of the time, Pallas kernels for 0%

profile of v1, /device:TPU:0, one launch (start us, length us, event | category | flops | bytes accessed | tf_op | source)
XLA Modules:
  0.0 183.2 jit_solution(11411019901324702024)
XLA Ops:
  7.2 5.1 %collective-permute-start = (bf16[256,1024]{1,0:T(8,128)(2,1)}, bf16[256,1024]{1,0:T(8,128)(2,1)S(1)}, u32[]{:S(2)}, u32[]{:S(2)}) collective-permute-start(bf16[256,1024]{1,0:T(8,128)(2,1)} %param.13), channel_id=1, source_target_pairs={{0,3},{1,0},{2,1},{3,2},{4,7},{5,4},{6,5},{7,6},{8,11},{9,8},{10,9... | collective-permute-start | bytes 1572872 | tf_op jit(solution)/shard_map/ppermute | solution.py:12
  18.2 5.6 %collective-permute-done = bf16[256,1024]{1,0:T(8,128)(2,1)S(1)} collective-permute-done((bf16[256,1024]{1,0:T(8,128)(2,1)}, bf16[256,1024]{1,0:T(8,128)(2,1)S(1)}, u32[]{:S(2)}, u32[]{:S(2)}) %collective-permute-start) | collective-permute-done | bytes 524320 | tf_op jit(solution)/shard_map/ppermute | solution.py:12
  23.9 2.1 %pad_maximum_fusion.1 = bf16[256,2048]{1,0:T(8,128)(2,1)} fusion(bf16[256,1024]{1,0:T(8,128)(2,1)S(1)} %collective-permute-done, bf16[256,1024]{1,0:T(8,128)(2,1)} %param.13), kind=kLoop, calls=%fused_computation.40 | loop fusion | flops 2097152 | bytes 2097152 | tf_op jit(solution)/shard_map/concatenate | solution.py:11
  30.1 1.6 copy.93
  31.7 1.6 copy.99
  35.7 1.6 copy.114
  40.0 2.2 %collective-permute-done.5 = f32[16]{0:T(128)} collective-permute-done((f32[16]{0:T(128)}, f32[16]{0:T(128)}, u32[]{:S(2)}, u32[]{:S(2)}) %collective-permute-start.5) | collective-permute-done | bytes 96 | tf_op jit(solution)/shard_map/ppermute | solution.py:30
  44.4 29.3 %collective-permute-done.1 = bf16[256,2048]{1,0:T(8,128)(2,1)S(1)} collective-permute-done((bf16[256,2048]{1,0:T(8,128)(2,1)}, bf16[256,2048]{1,0:T(8,128)(2,1)S(1)}, u32[]{:S(2)}, u32[]{:S(2)}) %collective-permute-start.1) | collective-permute-done | bytes 1048608 | tf_op jit(solution)/shard_map/ppermute | solution.py:12
  77.5 7.1 %fusion.21 = (f32[1024]{0:T(1024)}, bf16[256,1024]{1,0:T(8,128)(2,1)S(1)}, bf16[256,1024]{1,0:T(8,128)(2,1)S(1)}) fusion(bf16[256,1024]{1,0:T(8,128)(2,1)S(1)} %copy-done.8, f32[256,1024]{1,0:T(8,128)S(1)} %copy-done.5, bf16[1024,4096]{1,0:T(8,128)(2,1)} %param.22, bf16[256,8192]{1,0:T(8,128)(2,1)} %constant_dynamic-update-slice_fusion, s32[]{:T(128)S(6)} %select_n.87), kind=kOutput, calls=%fused_computation.36 | convolution fusion | flops 2149317632 | bytes 13111300 | tf_op jit(solution)/shard_map/dot_general | solution.py:60
  85.4 4.1 %fusion.1 = (f32[16,256]{1,0:T(8,128)}, f32[16,256]{1,0:T(8,128)}, bf16[256,256]{1,0:T(8,128)(2,1)S(1)}) fusion(f32[16,256]{1,0:T(8,128)} %copy-done.12, f32[256,256]{1,0:T(8,128)S(1)} %copy-done.10, pred[256,256]{1,0:T(8,128)(4,1)} %iota_compare_fusion, bf16[256,16,64]{0,2,1:T(8,128)(2,1)S(1)} %bitcast.111, f32[256,16,64]{0,2,1:T(8,128)S(1)} %bitcast.117, ...), kind=kOutput, calls=%fused_computation.7 | convolution fusion | flops 146202624 | bytes 2097152 | tf_op jit(solution)/shard_map/ihp,jhp->hij/dot_general | solution.py:81
  90.4 1.6 collective-permute-start.4
  92.0 2.3 %fusion.11 = f32[256,16,64]{0,2,1:T(8,128)} fusion(bf16[256,16,64]{0,2,1:T(8,128)(2,1)S(1)} %bitcast.112, f32[16,256]{1,0:T(8,128)S(1)} %copy-done.13, f32[256,256]{1,0:T(8,128)S(1)} %copy-done.11, pred[256,256]{1,0:T(8,128)(4,1)S(1)} %copy-done.14), kind=kOutput, calls=%fused_computation.21 | convolution fusion | flops 139460608 | bytes 1916928 | tf_op jit(solution)/shard_map/hij,ihp->jhp/dot_general | solution.py:83
  94.2 4.9 %collective-permute-done.4 = bf16[16,64,128]{2,1,0:T(8,128)(2,1)S(1)} collective-permute-done((bf16[16,64,128]{2,1,0:T(8,128)(2,1)S(1)}, bf16[16,64,128]{2,1,0:T(8,128)(2,1)S(1)}, u32[]{:S(2)}, u32[]{:S(2)}) %collective-permute-start.4) | collective-permute-done | bytes 262176 | tf_op jit(solution)/shard_map/ppermute | solution.py:31
  100.2 1.6 collective-permute-start.6
  102.3 5.8 %collective-permute-done.6 = bf16[16,64,128]{2,1,0:T(8,128)(2,1)S(1)} collective-permute-done((bf16[16,64,128]{2,1,0:T(8,128)(2,1)S(1)}, bf16[16,64,128]{2,1,0:T(8,128)(2,1)S(1)}, u32[]{:S(2)}, u32[]{:S(2)}) %collective-permute-start.6) | collective-permute-done | bytes 262176 | tf_op jit(solution)/shard_map/ppermute | solution.py:31
  109.7 2.7 %multiply_reduce_fusion.1 = (f32[256,16]{0,1:T(8,128)}, f32[256,16]{0,1:T(8,128)}, bf16[256,16,64]{0,2,1:T(8,128)(2,1)S(1)}) fusion(f32[256,1024]{0,1:T(8,128)S(1)} %copy.102, f32[256,16,64]{0,2,1:T(8,128)} %fusion.11, f32[256,16]{0,1:T(8,128)} %copy.114, bf16[256,1024]{0,1:T(8,128)(2,1)S(1)} %copy.94, f32[16]{0:T(128)} %param.20, f32[256,16]{0,1:T(8,128)} %copy.99, ...), kind=kOutput, calls=%fused_computation.42 | convolution fusion | flops 71950336 | bytes 4079811 | tf_op jit(solution)/shard_map/jn,hpn->jhp/dot_general | solution.py:99
  112.4 5.8 %fusion = bf16[4096,256]{0,1:T(8,128)(2,1)S(1)} fusion(bf16[256,1024]{0,1:T(8,128)(2,1)S(1)} %bitcast.132, bf16[4096,1024]{1,0:T(8,128)(2,1)} %param.23), kind=kOutput, calls=%fused_computation.1 | convolution fusion | flops 2148532224 | bytes 11010048 | tf_op jit(solution)/shard_map/dot_general | solution.py:130
  118.2 2.8 %reshape.138 = bf16[4,1024,256]{1,0,2:T(4,128)(2,1)} reshape(bf16[4096,256]{0,1:T(8,128)(2,1)S(1)} %fusion) | data formatting | bytes 4194304 | tf_op jit(solution)/shard_map/reshape | solution.py:136
  121.0 2.8 %pad_maximum_fusion = bf16[4,1088,256]{1,0,2:T(4,128)(2,1)S(1)} fusion(bf16[4,64,256]{1,0,2:T(4,128)(2,1)} %copy.105, bf16[4,1024,256]{1,0,2:T(4,128)(2,1)} %reshape.138), kind=kLoop, calls=%fused_computation.9 | loop fusion | flops 4456448 | bytes 4456448 | tf_op jit(solution)/shard_map/concatenate | solution.py:134
  123.8 3.6 %copy.106 = bf16[4,1088,256]{2,1,0:T(8,128)(2,1)} copy(bf16[4,1088,256]{1,0,2:T(4,128)(2,1)S(1)} %pad_maximum_fusion) | data formatting | bytes 4456448 | tf_op jit(solution)/shard_map/concatenate | solution.py:134
  138.1 2.1 %collective-permute-done.8 = f32[3,16]{1,0:T(4,128)S(1)} collective-permute-done((f32[3,16]{1,0:T(4,128)S(1)}, f32[3,16]{1,0:T(4,128)S(1)}, u32[]{:S(2)}, u32[]{:S(2)}) %collective-permute-start.8) | collective-permute-done | bytes 224 | tf_op jit(solution)/shard_map/ppermute | solution.py:49
  140.2 1.6 collective-permute-start.9
  144.5 28.7 %reduce-scatter.2.cloned.1.call-done = bf16[1088,256]{1,0:T(8,128)(2,1)} async-done(((bf16[4352,256]{1,0:T(8,128)(2,1)}), bf16[1088,256]{1,0:T(8,128)(2,1)}) %reduce-scatter.2.cloned.1.call-update) | async-done | bytes 557072 | tf_op jit(solution)/shard_map/reduce_scatter | solution.py:141
  173.1 1.9 %slice.49 = bf16[1024,256]{1,0:T(8,128)(2,1)} slice(bf16[1088,256]{1,0:T(8,128)(2,1)} %reduce-scatter.2.cloned.1.call-done), slice={[0:1024], [0:256]} | slice | bytes 1048576 | tf_op jit(solution)/shard_map/slice | solution.py:144
  (128 shorter events, 40.6 us)
Async XLA Ops:
  7.2 27.6 %copy-start = (bf16[256,128]{1,0:T(8,128)(2,1)S(1)}, bf16[256,128]{1,0:T(8,128)(2,1)}, u32[]{:S(2)}) copy-start(bf16[256,128]{1,0:T(8,128)(2,1)} %param.15) | copy-start | bytes 196612
  7.2 166.0 %reduce-scatter.2.cloned.1.call-start = ((), (), s32[]{:S(2)}) async-start(), calls=%async_computation.1 | async-start | bytes 2785280 | tf_op jit(solution)/shard_map/reduce_scatter | solution.py:141
  7.2 16.6 %collective-permute-start = (bf16[256,1024]{1,0:T(8,128)(2,1)}, bf16[256,1024]{1,0:T(8,128)(2,1)S(1)}, u32[]{:S(2)}, u32[]{:S(2)}) collective-permute-start(bf16[256,1024]{1,0:T(8,128)(2,1)} %param.13), channel_id=1, source_target_pairs={{0,3},{1,0},{2,1},{3,2},{4,7},{5,4},{6,5},{7,6},{8,11},{9,8},{10,9... | collective-permute-start | bytes 1572872 | tf_op jit(solution)/shard_map/ppermute | solution.py:12
  15.5 18.4 %copy-start.1 = (bf16[256,1024]{1,0:T(8,128)(2,1)S(1)}, bf16[256,1024]{1,0:T(8,128)(2,1)}, u32[]{:S(2)}) copy-start(bf16[256,1024]{1,0:T(8,128)(2,1)} %param.13) | copy-start | bytes 1572868
  16.2 21.1 %collective-permute-start.3 = (f32[16]{0:T(128)}, f32[16]{0:T(128)}, u32[]{:S(2)}, u32[]{:S(2)}) collective-permute-start(f32[16]{0:T(128)} %fusion.51), channel_id=1, source_target_pairs={{0,4},{4,0},{8,12},{12,8},{16,20},{20,16},{24,28},{28,24},{1,5},{5... | collective-permute-start | bytes 200 | tf_op jit(solution)/shard_map/ppermute | solution.py:30
  18.2 16.6 %copy-start.7 = (bf16[256,128]{1,0:T(8,128)(2,1)S(1)}, bf16[256,128]{1,0:T(8,128)(2,1)}, u32[]{:S(2)}) copy-start(bf16[256,128]{1,0:T(8,128)(2,1)} %param.16) | copy-start | bytes 196612
  26.0 47.6 %collective-permute-start.1 = (bf16[256,2048]{1,0:T(8,128)(2,1)}, bf16[256,2048]{1,0:T(8,128)(2,1)S(1)}, u32[]{:S(2)}, u32[]{:S(2)}) collective-permute-start(bf16[256,2048]{1,0:T(8,128)(2,1)} %pad_maximum_fusion.1), channel_id=1, source_target_pairs={{0,2},{1,3},{2,0},{3,1},{4,6},{5,7},{6,4},{7,5},{8,10},{9,11},{10,... | collective-permute-start | bytes 3145736 | tf_op jit(solution)/shard_map/ppermute | solution.py:12
  38.5 3.7 %collective-permute-start.5 = (f32[16]{0:T(128)}, f32[16]{0:T(128)}, u32[]{:S(2)}, u32[]{:S(2)}) collective-permute-start(f32[16]{0:T(128)} %fusion.52), channel_id=1, source_target_pairs={{0,8},{4,12},{8,0},{12,4},{16,24},{20,28},{24,16},{28,20},{1,9},{5... | collective-permute-start | bytes 200 | tf_op jit(solution)/shard_map/ppermute | solution.py:30
  40.0 37.5 %copy-start.5 = (f32[256,1024]{1,0:T(8,128)S(1)}, f32[256,1024]{1,0:T(8,128)}, u32[]{:S(2)}) copy-start(f32[256,1024]{1,0:T(8,128)} %copy.103) | copy-start | bytes 3145732
  40.0 37.5 %copy-start.8 = (bf16[256,1024]{1,0:T(8,128)(2,1)S(1)}, bf16[256,1024]{1,0:T(8,128)(2,1)}, u32[]{:S(2)}) copy-start(bf16[256,1024]{1,0:T(8,128)(2,1)} %param.14) | copy-start | bytes 1572868
  77.5 7.9 %copy-start.10 = (f32[256,256]{1,0:T(8,128)S(1)}, f32[256,256]{1,0:T(8,128)}, u32[]{:S(2)}) copy-start(f32[256,256]{1,0:T(8,128)} %fusion.59) | copy-start | bytes 786436
  85.0 24.7 %copy-start.2 = (bf16[256,1024]{0,1:T(8,128)(2,1)}, bf16[256,1024]{0,1:T(8,128)(2,1)S(1)}, u32[]{:S(2)}) copy-start(bf16[256,1024]{0,1:T(8,128)(2,1)S(1)} %copy.94) | copy-start | bytes 1572868
  85.3 4.2 %collective-permute-start.2 = (bf16[16,64,128]{2,1,0:T(8,128)(2,1)S(1)}, bf16[16,64,128]{2,1,0:T(8,128)(2,1)S(1)}, u32[]{:S(2)}, u32[]{:S(2)}) collective-permute-start(bf16[16,64,128]{2,1,0:T(8,128)(2,1)S(1)} %get-tuple-element.48), channel_id=1, source_target_pairs={{0,4},{4,0},{8,12},{12,8},{16,20},{20,16},{24,28},{28,24},{1,5},{5... | collective-permute-start | bytes 786440 | tf_op jit(solution)/shard_map/ppermute | solution.py:31
  90.3 11.4 %copy-start.4 = (bf16[1,1024,128]{2,1,0:T(8,128)(2,1)S(1)}, bf16[1,1024,128]{2,1,0:T(8,128)(2,1)}, u32[]{:S(2)}) copy-start(bf16[1,1024,128]{2,1,0:T(8,128)(2,1)} %param.21) | copy-start | bytes 786436
  90.4 17.7 %copy-start.16 = (f32[256,16]{0,1:T(8,128)S(1)}, f32[256,16]{0,1:T(8,128)}, u32[]{:S(2)}) copy-start(f32[256,16]{0,1:T(8,128)} %copy.99) | copy-start | bytes 49156
  90.4 17.7 %copy-start.19 = (f32[16]{0:T(128)S(1)}, f32[16]{0:T(128)}, u32[]{:S(2)}) copy-start(f32[16]{0:T(128)} %get-tuple-element.35) | copy-start | bytes 196
  90.4 17.7 %copy-start.20 = (f32[16]{0:T(128)S(1)}, f32[16]{0:T(128)}, u32[]{:S(2)}) copy-start(f32[16]{0:T(128)} %get-tuple-element.36) | copy-start | bytes 196
  90.4 8.7 %collective-permute-start.4 = (bf16[16,64,128]{2,1,0:T(8,128)(2,1)S(1)}, bf16[16,64,128]{2,1,0:T(8,128)(2,1)S(1)}, u32[]{:S(2)}, u32[]{:S(2)}) collective-permute-start(bf16[16,64,128]{2,1,0:T(8,128)(2,1)S(1)} %fusion.54), channel_id=1, source_target_pairs={{0,8},{4,12},{8,0},{12,4},{16,24},{20,28},{24,16},{28,20},{1,9},{5... | collective-permute-start | bytes 786440 | tf_op jit(solution)/shard_map/ppermute | solution.py:31
  94.2 15.4 %copy-start.15 = (f32[256,16]{0,1:T(8,128)S(1)}, f32[256,16]{0,1:T(8,128)}, u32[]{:S(2)}) copy-start(f32[256,16]{0,1:T(8,128)} %copy.93) | copy-start | bytes 49156
  99.1 13.2 %copy-start.6 = (bf16[16,64,128]{2,1,0:T(8,128)(2,1)}, bf16[16,64,128]{2,1,0:T(8,128)(2,1)S(1)}, u32[]{:S(2)}) copy-start(bf16[16,64,128]{2,1,0:T(8,128)(2,1)S(1)} %collective-permute-done.4) | copy-start | bytes 786436
  100.2 7.9 %collective-permute-start.6 = (bf16[16,64,128]{2,1,0:T(8,128)(2,1)S(1)}, bf16[16,64,128]{2,1,0:T(8,128)(2,1)S(1)}, u32[]{:S(2)}, u32[]{:S(2)}) collective-permute-start(bf16[16,64,128]{2,1,0:T(8,128)(2,1)S(1)} %fusion.29), channel_id=1, source_target_pairs={{0,16},{4,20},{8,24},{12,28},{16,0},{20,4},{24,8},{28,12},{1,17},{... | collective-permute-start | bytes 786440 | tf_op jit(solution)/shard_map/ppermute | solution.py:31
  135.3 1.2 collective-permute-start.7
  136.6 3.7 %collective-permute-start.8 = (f32[3,16]{1,0:T(4,128)S(1)}, f32[3,16]{1,0:T(4,128)S(1)}, u32[]{:S(2)}, u32[]{:S(2)}) collective-permute-start(f32[3,16]{1,0:T(4,128)S(1)} %fusion.53), channel_id=1, source_target_pairs={{0,8},{4,12},{8,0},{12,4},{16,24},{20,28},{24,16},{28,20},{1,9},{5... | collective-permute-start | bytes 584 | tf_op jit(solution)/shard_map/ppermute | solution.py:49
  140.2 3.7 %collective-permute-start.9 = (f32[3,16]{1,0:T(4,128)S(1)}, f32[3,16]{1,0:T(4,128)S(1)}, u32[]{:S(2)}, u32[]{:S(2)}) collective-permute-start(f32[3,16]{1,0:T(4,128)S(1)} %fusion.74), channel_id=1, source_target_pairs={{0,16},{4,20},{8,24},{12,28},{16,0},{20,4},{24,8},{28,12},{1,17},{... | collective-permute-start | bytes 584 | tf_op jit(solution)/shard_map/ppermute | solution.py:49
  (12 other events, 53.1 us)
Sparse Core Ops, SparseCore 0:
  127.5 45.5 reduce-scatter.1
